TPU v7x, 32 devices: a whole 2x2x4 slice. The times are simulated.
32 devices in a mesh: group: 2 (over y), tile: 4 (over x, core), seq: 4 (over z).
Axes of the slice: x: 2, y: 2, z: 4, core: 2. Of those that a mesh axis runs over, the one named last changes fastest.
Arguments:
- hidden: bfloat16 [8, 1024, 3072], P(('group', 'tile'), 'seq'), parts along dimension 0
- modulation: float32 [10, 3072], P('group'), parts along dimension 0, may hold values from -3 to 3
- w_qkv: bfloat16 [3072, 9216], P('tile', 'seq')
- w_out: bfloat16 [3072, 3072], P('seq', 'tile'), may hold values from -0.109375 to 0.109375
- w_head: bfloat16 [3072, 64], replicated, may hold values from -0.109375 to 0.109375
- latent: float32 [8, 1024, 64], P(('group', 'tile'), 'seq'), parts along dimension 0, may hold values from -6 to 6
- weights_int: int32 [8, 1024], P(('group', 'tile'), 'seq'), parts along dimension 0, may hold values from 1 to 8
- step_index: int32 [2], P('group'), parts along dimension 0, may hold values from 0 to 13
Outputs:
- stepped: float32 [8, 1024, 64], P(('group', 'tile'), 'seq'), parts along dimension 0
- clean: float32 [8, 1024, 64], P(('group', 'tile'), 'seq'), parts along dimension 0
There are 2 independent parts, one for each index of `group`. A program takes and returns all parts, laid end to end along the dimension named above; an argument that names none is the same for every part. Nothing has to cross between parts.
All inputs are finite; a program needn't handle non-finite values.
Results may differ from a plain program's by a relative error of at most 0.0055.
Values may be sent and summed in bfloat16 or wider, within the bound.
A program may use at most 64 MiB of HBM per device.

v0:
```python
import math
import jax
import jax.numpy as jnp
from jax import lax
from jax.sharding import PartitionSpec as P

HD = 128
NSTEPS = 28


def shifted(value, axis, steps):
    count = lax.axis_size(axis)
    leading, last = (max(0, -steps), min(count, count - steps))
    return lax.ppermute(value, axis, [(source, source + steps) for source in range(leading, last)])


def layer_norm(values):
    mean = jnp.mean(values, axis=-1, keepdims=True)
    centred = values - mean
    spread = jnp.mean(centred * centred, axis=-1, keepdims=True)
    return centred * lax.rsqrt(spread + 1e-06)


def root_norm(values):
    return values * lax.rsqrt(jnp.mean(values * values, axis=-1, keepdims=True) + 1e-06)


def noise_level(index, steps):
    level = 1.0 - index / steps
    return 3.0 * level / (1.0 + 2.0 * level)


def shards(hidden, modulation, w_qkv, w_out, w_head, latent, weights_int, step_index):
    local = hidden[0].astype(jnp.float32)
    norm_in = (layer_norm(local) * (1.0 + modulation[1]) + modulation[0]).astype(jnp.bfloat16)
    gathered = lax.all_gather(norm_in, "seq", axis=0, tiled=True)
    length = gathered.shape[0]
    heads_here = w_qkv.shape[1] // (3 * HD)
    projected = jnp.dot(
        gathered,
        lax.all_gather(w_qkv, "tile", axis=0, tiled=True),
        preferred_element_type=jnp.float32,
    )
    full_out = lax.all_gather(w_out, "tile", axis=1, tiled=True)
    projected = projected.reshape(length, heads_here, 3, HD)
    queries = root_norm(projected[:, :, 0]).astype(jnp.bfloat16)
    keys = root_norm(projected[:, :, 1]).astype(jnp.bfloat16)
    values = projected[:, :, 2].astype(jnp.bfloat16)
    block = min(512, length)
    scale = 1.0 / math.sqrt(HD)
    pieces = []
    for first in range(0, length, block):
        scores = (
            jnp.einsum(
                "qhe,khe->hqk",
                queries[first : first + block],
                keys,
                preferred_element_type=jnp.float32,
            )
            * scale
        )
        expo = jnp.exp(scores)
        probs = (expo / jnp.sum(expo, axis=-1, keepdims=True)).astype(jnp.bfloat16)
        pieces.append(
            jnp.einsum("hqk,khe->qhe", probs, values, preferred_element_type=jnp.float32).astype(
                jnp.bfloat16
            )
        )
    attended = jnp.concatenate(pieces, axis=0).reshape(length, heads_here * HD)
    summed = lax.psum_scatter(
        jnp.dot(attended, full_out, preferred_element_type=jnp.float32).astype(jnp.bfloat16),
        "seq",
        scatter_dimension=0,
        tiled=True,
    ).astype(jnp.float32)
    mixed = local + modulation[2] * summed
    norm_out = (layer_norm(mixed) * (1.0 + modulation[4]) + modulation[3]).astype(jnp.bfloat16)
    velocity = jnp.dot(norm_out, w_head, preferred_element_type=jnp.float32)
    index = step_index[0].astype(jnp.float32)
    now = noise_level(index, NSTEPS)
    after = noise_level(index + 1.0, NSTEPS)
    base = latent[0]
    weight = weights_int[0].astype(jnp.float32)
    moved = base + (after - now) * velocity
    guess = base - now * velocity
    weighted = jnp.concatenate([moved, guess], axis=1) * weight[:, None]
    seq_count = lax.axis_size("seq")
    place = lax.axis_index("seq")
    prev_tile = (
        shifted(weighted.astype(jnp.bfloat16), "tile", 1).astype(weighted.dtype),
        shifted(weight.astype(jnp.bfloat16), "tile", 1).astype(weight.dtype),
    )
    prev_sums, prev_weight = (
        shifted(prev_tile[0].astype(jnp.bfloat16), "seq", -(seq_count - 2)).astype(jnp.float32),
        shifted(prev_tile[1].astype(jnp.bfloat16), "seq", -(seq_count - 2)).astype(jnp.float32),
    )
    next_tile = (
        shifted(weighted.astype(jnp.bfloat16), "tile", -1).astype(weighted.dtype),
        shifted(weight.astype(jnp.bfloat16), "tile", -1).astype(weight.dtype),
    )
    next_sums, next_weight = (
        shifted(next_tile[0].astype(jnp.bfloat16), "seq", seq_count - 2).astype(jnp.float32),
        shifted(next_tile[1].astype(jnp.bfloat16), "seq", seq_count - 2).astype(jnp.float32),
    )
    take_prev = place < 2
    take_next = place >= seq_count - 2
    totals = weighted + jnp.where(take_prev, prev_sums, 0.0) + jnp.where(take_next, next_sums, 0.0)
    norms = weight + jnp.where(take_prev, prev_weight, 0.0) + jnp.where(take_next, next_weight, 0.0)
    joined = totals / norms[:, None]
    channels = velocity.shape[1]
    return (joined[None, :, :channels], joined[None, :, channels:])


def solution(mesh):
    in_specs = (
        P(("group", "tile"), "seq", None),
        P("group", None),
        P("tile", "seq"),
        P("seq", "tile"),
        P(),
        P(("group", "tile"), "seq", None),
        P(("group", "tile"), "seq"),
        P("group"),
    )
    out_specs = (P(("group", "tile"), "seq", None), P(("group", "tile"), "seq", None))
    return jax.shard_map(shards, mesh=mesh, in_specs=in_specs, out_specs=out_specs, check_vma=False)
```

profile of v0, /device:TPU:26, one launch (start us, length us, event | category | flops | bytes accessed | tf_op | source)
XLA Modules:
  0.0 437.2 jit_solution(16859526870282650366)
XLA Ops:
  7.2 0.0 copy-start
  7.2 0.0 copy-start.1
  7.2 0.0 all-gather.4.cloned.1.call-start
  7.2 1.9 fusion.30
  9.1 1.7 convert_reduce_fusion
  10.8 2.0 fusion.8
  12.8 0.0 copy-done.1
  12.8 1.9 fusion.11
  14.7 0.0 all-gather.4.cloned.1.call-update
  14.8 0.0 all-gather.6.cloned.1.call-start
  14.8 0.7 all-gather.6.cloned.1.call-update
  15.5 0.0 all-gather.8.cloned.1.call-start
  15.6 0.7 all-gather.8.cloned.1.call-update
  16.3 0.0 reduce-scatter.2.cloned.1.call-start
  16.3 112.1 %all-gather.4.cloned.1.call-done = bf16[1024,3072]{1,0:T(8,128)(2,1)} async-done(((bf16[256,3072]{1,0:T(8,128)(2,1)}), bf16[1024,3072]{1,0:T(8,128)(2,1)}) %all-gather.4.cloned.1.call-update) | async-done | bytes 6291472 | tf_op jit(solution)/shard_map/all_gather | solution.py:36
  128.4 92.7 %all-gather.6.cloned.1.call-done = bf16[3072,2304]{1,0:T(8,128)(2,1)} async-done(((bf16[768,2304]{1,0:T(8,128)(2,1)}), bf16[3072,2304]{1,0:T(8,128)(2,1)}) %all-gather.6.cloned.1.call-update) | async-done | bytes 14155792 | tf_op jit(solution)/shard_map/all_gather | solution.py:41
  221.1 19.6 %fusion.31 = f32[1024,2304]{0,1:T(8,128)S(1)} fusion(bf16[1024,3072]{1,0:T(8,128)(2,1)} %all-gather.4.cloned.1.call-done, bf16[3072,2304]{1,0:T(8,128)(2,1)} %all-gather.6.cloned.1.call-done), kind=kOutput, calls=%fused_computation.60 | convolution fusion | flops 14495514624 | bytes 29884416 | tf_op jit(solution)/shard_map/dot_general | solution.py:39
  240.7 0.0 copy-start.3
  240.7 3.5 copy-done.3
  244.2 2.0 slice.50
  246.3 3.6 copy.21
  249.9 2.9 fusion.12
  252.8 2.3 multiply_reduce_fusion.1
  255.2 0.0 copy-done.2
  255.2 0.0 slice-start
  255.2 1.0 fusion.13
  256.2 0.0 slice-start.1
  256.2 0.0 slice-start.2
  256.2 8.2 %fusion = (f32[6,512]{1,0:T(8,128)S(1)}, f32[6,512,1024]{2,1,0:T(8,128)}) fusion(f32[1024,6,3,128]{0,3,2,1:T(8,128)} %bitcast.78, f32[1024,6]{0,1:T(8,128)S(1)} %add_rsqrt_fusion, bf16[1024,6,128]{2,0,1:T(8,128)(2,1)S(1)} %fusion.13), kind=kOutput, calls=%fused_computation.4 | convolution fusion | flops 813167616 | bytes 16560128 | tf_op jit(solution)/shard_map/qhe,khe->hqk/dot_general | solution.py:54
  264.4 0.0 slice-done
  264.4 0.0 slice-done.1
  264.4 0.0 slice-done.2
  264.5 2.7 fusion.1
  267.1 6.0 %fusion.19 = bf16[512,6,128]{0,2,1:T(8,128)(2,1)S(1)} fusion(f32[6,512,1024]{2,1,0:T(8,128)} %get-tuple-element.14, f32[6,512]{1,0:T(8,128)S(1)} %get-tuple-element.13, f32[1024,6,3,128]{0,3,2,1:T(8,128)S(1)} %bitcast.82), kind=kOutput, calls=%fused_computation.35 | convolution fusion | flops 815136768 | bytes 14958592 | tf_op jit(solution)/shard_map/hqk,khe->qhe/dot_general | solution.py:65
  273.1 2.9 fusion.20
  276.1 0.2 pad_maximum_fusion
  276.3 0.0 all-gather.8.cloned.1.call-done
  276.3 9.5 %convolution_convert_fusion = bf16[1024,3072]{1,0:T(8,128)(2,1)} fusion(bf16[1024,768]{0,1:T(8,128)(2,1)S(1)} %bitcast.84, bf16[768,3072]{1,0:T(8,128)(2,1)} %all-gather.8.cloned.1.call-done), kind=kOutput, calls=%fused_computation.8 | convolution fusion | flops 4834983936 | bytes 12582912 | tf_op jit(solution)/shard_map/dot_general | solution.py:71
  285.9 0.0 reduce-scatter.2.cloned.1.call-update
  286.5 0.0 copy-done.7
  286.6 110.6 %reduce-scatter.2.cloned.1.call-done = bf16[256,3072]{1,0:T(8,128)(2,1)} async-done(((bf16[1024,3072]{1,0:T(8,128)(2,1)}), bf16[256,3072]{1,0:T(8,128)(2,1)}) %reduce-scatter.2.cloned.1.call-update) | async-done | bytes 1572880 | tf_op jit(solution)/shard_map/reduce_scatter | solution.py:70
  397.2 2.1 fusion.14
  399.4 0.8 multiply_reduce_fusion
  400.2 0.0 copy-done.5
  400.2 0.0 copy-done.6
  400.2 0.0 copy-done.8
  400.2 1.1 bitcast_add_fusion
  401.3 1.9 collective-permute-start
  403.3 3.6 collective-permute-start.2
  406.9 1.9 collective-permute-start.4
  408.9 3.6 collective-permute-start.6
  412.5 0.0 collective-permute-done.4
  412.5 2.9 collective-permute-start.5
  415.5 0.0 collective-permute-done.6
  415.5 1.3 collective-permute-start.7
  416.8 0.0 collective-permute-done
  416.8 5.4 %collective-permute-start.1 = (bf16[256,128]{0,1:T(8,128)(2,1)S(1)}, bf16[256,128]{0,1:T(8,128)(2,1)S(1)}, u32[]{:S(2)}, u32[]{:S(2)}) collective-permute-start(bf16[256,128]{0,1:T(8,128)(2,1)S(1)} %collective-permute-done), channel_id=1, source_target_pairs={{2,0},{3,1},{6,4},{7,5},{10,8},{11,9},{14,12},{15,13},{18,16},{19,... | collective-permute-start | bytes 196616 | tf_op jit(solution)/shard_map/ppermute | solution.py:14
  422.2 0.0 collective-permute-done.2
  422.2 1.3 collective-permute-start.3
  423.5 0.0 collective-permute-done.5
  423.6 0.0 collective-permute-done.7
  423.6 0.5 collective-permute-done.1
  424.1 5.9 %collective-permute-done.3 = bf16[256,128]{0,1:T(8,128)(2,1)S(1)} collective-permute-done((bf16[256,128]{0,1:T(8,128)(2,1)S(1)}, bf16[256,128]{0,1:T(8,128)(2,1)S(1)}, u32[]{:S(2)}, u32[]{:S(2)}) %collective-permute-start.3) | collective-permute-done | bytes 65568 | tf_op jit(solution)/shard_map/ppermute | solution.py:14
  430.0 0.7 slice_bitcast_fusion.1
  (20 shorter events, 0.1 us)
Async XLA Ops:
  7.2 393.0 %copy-start = (bf16[3072,64]{0,1:T(8,128)(2,1)S(1)}, bf16[3072,64]{0,1:T(8,128)(2,1)}, u32[]{:S(2)}) copy-start(bf16[3072,64]{0,1:T(8,128)(2,1)} %param.12) | copy-start | bytes 1179652
  7.2 5.6 %copy-start.1 = (bf16[1,256,3072]{2,1,0:T(8,128)(2,1)S(1)}, bf16[1,256,3072]{2,1,0:T(8,128)(2,1)}, u32[]{:S(2)}) copy-start(bf16[1,256,3072]{2,1,0:T(8,128)(2,1)} %param.8) | copy-start | bytes 4718596
  7.2 121.2 %all-gather.4.cloned.1.call-start = ((), (), s32[]{:S(2)}) async-start(), calls=%async_computation.1 | async-start | bytes 7864320 | tf_op jit(solution)/shard_map/all_gather | solution.py:36
  14.8 206.3 %all-gather.6.cloned.1.call-start = ((), (), s32[]{:S(2)}) async-start(), calls=%async_computation.2 | async-start | bytes 17694720 | tf_op jit(solution)/shard_map/all_gather | solution.py:41
  15.5 260.8 %all-gather.8.cloned.1.call-start = ((), (), s32[]{:S(2)}) async-start(), calls=%async_computation.3 | async-start | bytes 5898240 | tf_op jit(solution)/shard_map/all_gather | solution.py:44
  16.3 381.0 %reduce-scatter.2.cloned.1.call-start = ((), (), s32[]{:S(2)}) async-start(), calls=%async_computation.4 | async-start | bytes 7864320 | tf_op jit(solution)/shard_map/reduce_scatter | solution.py:70
  240.7 3.6 copy-start.3
  249.9 5.3 %copy-start.2 = (f32[1024,6,1,128]{3,0,1,2:T(8,128)S(1)}, f32[1024,6,1,128]{3,0,1,2:T(8,128)}, u32[]{:S(2)}) copy-start(f32[1024,6,1,128]{3,0,1,2:T(8,128)} %copy.21) | copy-start | bytes 9437188
  255.2 9.2 %slice-start = ((s8[9437184]{0:T(1024)(128)(4,1)}), s8[4194304]{0:T(1024)(128)(4,1)S(1)}, s32[]{:S(2)}) async-start(s8[9437184]{0:T(1024)(128)(4,1)} %bitcast.79), calls=%async_computation.5 | async-start | bytes 8388608
  256.2 8.3 %slice-start.1 = ((s8[9437184]{0:T(1024)(128)(4,1)}), s8[4194304]{0:T(1024)(128)(4,1)S(1)}, s32[]{:S(2)}) async-start(s8[9437184]{0:T(1024)(128)(4,1)} %bitcast.79), calls=%async_computation.6 | async-start | bytes 8388608
  256.2 8.2 %slice-start.2 = ((s8[9437184]{0:T(1024)(128)(4,1)}), s8[1048576]{0:T(1024)(128)(4,1)S(1)}, s32[]{:S(2)}) async-start(s8[9437184]{0:T(1024)(128)(4,1)} %bitcast.79), calls=%async_computation.7 | async-start | bytes 2097152
  285.8 0.7 copy-start.7
  397.2 2.1 copy-start.4
  397.2 3.0 copy-start.5
  397.2 3.0 copy-start.6
  397.2 3.0 copy-start.8
  401.3 15.4 %collective-permute-start = (bf16[256,128]{0,1:T(8,128)(2,1)S(1)}, bf16[256,128]{0,1:T(8,128)(2,1)S(1)}, u32[]{:S(2)}, u32[]{:S(2)}) collective-permute-start(bf16[256,128]{0,1:T(8,128)(2,1)S(1)} %fusion.27), channel_id=1, source_target_pairs={{0,4},{4,8},{8,12},{1,5},{5,9},{9,13},{2,6},{6,10},{10,14},{3,7},{... | collective-permute-start | bytes 196616 | tf_op jit(solution)/shard_map/ppermute | solution.py:14
  403.3 19.0 %collective-permute-start.2 = (bf16[256,128]{0,1:T(8,128)(2,1)S(1)}, bf16[256,128]{0,1:T(8,128)(2,1)S(1)}, u32[]{:S(2)}, u32[]{:S(2)}) collective-permute-start(bf16[256,128]{0,1:T(8,128)(2,1)S(1)} %fusion.27), channel_id=1, source_target_pairs={{4,0},{8,4},{12,8},{5,1},{9,5},{13,9},{6,2},{10,6},{14,10},{7,3},{... | collective-permute-start | bytes 196616 | tf_op jit(solution)/shard_map/ppermute | solution.py:14
  406.9 5.6 %collective-permute-start.4 = (bf16[256]{0:T(256)(128)(2,1)S(1)}, bf16[256]{0:T(256)(128)(2,1)S(1)}, u32[]{:S(2)}, u32[]{:S(2)}) collective-permute-start(bf16[256]{0:T(256)(128)(2,1)S(1)} %convert_element_type.109), channel_id=1, source_target_pairs={{0,4},{4,8},{8,12},{1,5},{5,9},{9,13},{2,6},{6,10},{10,14},{3,7},{... | collective-permute-start | bytes 1544 | tf_op jit(solution)/shard_map/ppermute | solution.py:14
  408.9 6.6 %collective-permute-start.6 = (bf16[256]{0:T(256)(128)(2,1)S(1)}, bf16[256]{0:T(256)(128)(2,1)S(1)}, u32[]{:S(2)}, u32[]{:S(2)}) collective-permute-start(bf16[256]{0:T(256)(128)(2,1)S(1)} %convert_element_type.109), channel_id=1, source_target_pairs={{4,0},{8,4},{12,8},{5,1},{9,5},{13,9},{6,2},{10,6},{14,10},{7,3},{... | collective-permute-start | bytes 1544 | tf_op jit(solution)/shard_map/ppermute | solution.py:14
  412.5 11.0 %collective-permute-start.5 = (bf16[256]{0:T(256)(128)(2,1)S(1)}, bf16[256]{0:T(256)(128)(2,1)S(1)}, u32[]{:S(2)}, u32[]{:S(2)}) collective-permute-start(bf16[256]{0:T(256)(128)(2,1)S(1)} %collective-permute-done.4), channel_id=1, source_target_pairs={{2,0},{3,1},{6,4},{7,5},{10,8},{11,9},{14,12},{15,13},{18,16},{19,... | collective-permute-start | bytes 1544 | tf_op jit(solution)/shard_map/ppermute | solution.py:14
  415.5 8.1 %collective-permute-start.7 = (bf16[256]{0:T(256)(128)(2,1)S(1)}, bf16[256]{0:T(256)(128)(2,1)S(1)}, u32[]{:S(2)}, u32[]{:S(2)}) collective-permute-start(bf16[256]{0:T(256)(128)(2,1)S(1)} %collective-permute-done.6), channel_id=1, source_target_pairs={{0,2},{1,3},{4,6},{5,7},{8,10},{9,11},{12,14},{13,15},{16,18},{17,... | collective-permute-start | bytes 1544 | tf_op jit(solution)/shard_map/ppermute | solution.py:14
  416.8 7.3 %collective-permute-start.1 = (bf16[256,128]{0,1:T(8,128)(2,1)S(1)}, bf16[256,128]{0,1:T(8,128)(2,1)S(1)}, u32[]{:S(2)}, u32[]{:S(2)}) collective-permute-start(bf16[256,128]{0,1:T(8,128)(2,1)S(1)} %collective-permute-done), channel_id=1, source_target_pairs={{2,0},{3,1},{6,4},{7,5},{10,8},{11,9},{14,12},{15,13},{18,16},{19,... | collective-permute-start | bytes 196616 | tf_op jit(solution)/shard_map/ppermute | solution.py:14
  422.2 7.7 %collective-permute-start.3 = (bf16[256,128]{0,1:T(8,128)(2,1)S(1)}, bf16[256,128]{0,1:T(8,128)(2,1)S(1)}, u32[]{:S(2)}, u32[]{:S(2)}) collective-permute-start(bf16[256,128]{0,1:T(8,128)(2,1)S(1)} %collective-permute-done.2), channel_id=1, source_target_pairs={{0,2},{1,3},{4,6},{5,7},{8,10},{9,11},{12,14},{13,15},{16,18},{17,... | collective-permute-start | bytes 196616 | tf_op jit(solution)/shard_map/ppermute | solution.py:14
Sparse Core Ops, SparseCore 0:
  14.9 113.4 all-gather.3
  129.9 91.1 all-gather.5
  222.6 37.4 all-gather.7
  286.0 111.1 reduce-scatter.1
where the time goes:
time: 438 us; the launch traced here: 437 us
  waiting for transfers between devices  323 us (74%)
  matrix products  50 us (11%)
  starting transfers between devices  22.2 us (5%)
  other arithmetic  17 us (4%)
  between operations  14.9 us (3%)
  local copies, waits for them, and re-layouts  9.9 us (2%)
    all_gather x1, waiting for transfers between devices, shards(): gathered = lax.all_gather(norm_in, 'seq', axis=0, tiled=True)  112 us
    reduce_scatter x1, waiting for transfers between devices, shards(): lax.psum_scatter(jnp.dot(attended, full_out, preferred_element_type=jnp.f...  111 us
    all_gather x1, waiting for transfers between devices, shards(): lax.all_gather(w_qkv, 'tile', axis=0, tiled=True)  92.7 us
    ppermute x8, starting transfers between devices, shifted(): lax.ppermute(value, axis, [(source, source + steps) for source in range(l...  22.1 us
    dot_general x1, matrix products, shards(): jnp.dot(gathered, lax.all_gather(w_qkv, 'tile', axis=0, tiled=True), pref...  19.6 us
    dot_general x2, matrix products, shards(): jnp.einsum('qhe,khe->hqk', queries[first:first + block], keys, preferred_...  10.9 us
    dot_general x1, matrix products, shards(): jnp.dot(attended, full_out, preferred_element_type=jnp.float32)  9.54 us
    dot_general x2, matrix products, shards(): jnp.einsum('hqk,khe->qhe', probs, values, preferred_element_type=jnp.floa...  8.92 us
  transfers between devices with their start and end apart: 12, of which 5 were waited for; matrix products, arithmetic and copies ran while one was open for 12% of the time, Pallas kernels for 0%

commit v1 on v0

--- a/solution.py
+++ b/solution.py
@@ -3,9 +3,29 @@
 import jax.numpy as jnp
 from jax import lax
 from jax.sharding import PartitionSpec as P
+from jax.lax import axis_index, axis_size, ppermute
 
 HD = 128
 NSTEPS = 28
+
+
+def map_the_figure(s0, shard_axis):
+    trail = []
+    c = 1
+    count_all = axis_size(shard_axis)
+    while c < count_all:
+        trail.append((c - 1, c))
+        c += 1
+    y_new = s0
+    gallery = [y_new]
+    k = 0
+    local_out = trail + [(count_all - 1, 0)]
+    while k < count_all - 1:
+        y_new = ppermute(y_new, axis_name=shard_axis, perm=local_out)
+        gallery += [y_new]
+        k += 1
+    high = jnp.concatenate([*reversed(gallery)], axis=0)
+    return jnp.roll(high, (axis_index(shard_axis) + 1) * y_new.shape[0], 0)
 
 
 def shifted(value, axis, steps):
@@ -33,7 +53,7 @@
 def shards(hidden, modulation, w_qkv, w_out, w_head, latent, weights_int, step_index):
     local = hidden[0].astype(jnp.float32)
     norm_in = (layer_norm(local) * (1.0 + modulation[1]) + modulation[0]).astype(jnp.bfloat16)
-    gathered = lax.all_gather(norm_in, "seq", axis=0, tiled=True)
+    gathered = map_the_figure(norm_in, "seq")
     length = gathered.shape[0]
     heads_here = w_qkv.shape[1] // (3 * HD)
     projected = jnp.dot(

time: 438 us -> 352 us (0.80)
  waiting for transfers between devices: 323 us -> 221 us
  local copies, waits for them, and re-layouts: 9.9 us -> 23.8 us
    all_gather x1 -> x0, waiting for transfers between devices: 112 us -> none  [shards(): gathered = lax.all_gather(norm_in, 'seq', axis=0, tiled=True)]
    ppermute x0 -> x3, waiting for transfers between devices: none -> 102 us  [map_the_figure(): y_new = ppermute(y_new, axis_name=shard_axis, perm=local_out)]
    all_gather x1, waiting for transfers between devices: 92.7 us -> 0.01 us  [shards(): lax.all_gather(w_qkv, 'tile', axis=0, tiled=True)]
    unnamed x25 -> x43, local copies, waits for them, and re-layouts: 7.19 us -> 21 us
    ppermute x0 -> x3, starting transfers between devices: none -> 6.19 us  [map_the_figure(): y_new = ppermute(y_new, axis_name=shard_axis, perm=local_out)]
  transfers between devices with their start and end apart: 12 -> 14, of which waited for: 5 -> 7; matrix products, arithmetic and copies ran while one was open for 12% -> 20% of each run, Pallas kernels for 0% -> 0%
where the time goes in v1:
time: 352 us; the launch traced here: 350 us
  waiting for transfers between devices  221 us (63%)
  matrix products  50.1 us (14%)
  starting transfers between devices  24.4 us (7%)
  local copies, waits for them, and re-layouts  23.8 us (7%)
  other arithmetic  15.7 us (4%)
  between operations  14.9 us (4%)
    reduce_scatter x1, waiting for transfers between devices, shards(): lax.psum_scatter(jnp.dot(attended, full_out, preferred_element_type=jnp.f...  112 us
    ppermute x3, waiting for transfers between devices, map_the_figure(): y_new = ppermute(y_new, axis_name=shard_axis, perm=local_out)  102 us
    unnamed x43, local copies, waits for them, and re-layouts  21 us
    dot_general x1, matrix products, shards(): jnp.dot(gathered, lax.all_gather(w_qkv, 'tile', axis=0, tiled=True), pref...  19.6 us
    ppermute x8, starting transfers between devices, shifted(): lax.ppermute(value, axis, [(source, source + steps) for source in range(l...  18 us
    dot_general x2, matrix products, shards(): jnp.einsum('qhe,khe->hqk', queries[first:first + block], keys, preferred_...  10.9 us
    dot_general x1, matrix products, shards(): jnp.dot(attended, full_out, preferred_element_type=jnp.float32)  9.61 us
    dot_general x2, matrix products, shards(): jnp.einsum('hqk,khe->qhe', probs, values, preferred_element_type=jnp.floa...  8.92 us
  transfers between devices with their start and end apart: 14, of which 7 were waited for; matrix products, arithmetic and copies ran while one was open for 20% of the time, Pallas kernels for 0%

profile of v1, /device:TPU:26, one launch (start us, length us, event | category | flops | bytes accessed | tf_op | source)
XLA Modules:
  0.0 349.6 jit_solution(17918566632560923291)
XLA Ops:
  7.2 0.0 copy-start
  7.2 0.0 all-gather.3.cloned.1.call-start
  7.2 0.7 all-gather.3.cloned.1.call-update
  7.9 0.0 all-gather.5.cloned.1.call-start
  8.0 0.7 copy-done.1
  8.6 0.3 convert_reduce_fusion
  8.9 0.6 fusion.10
  9.5 0.7 fusion.33
  10.2 0.8 fusion.13
  11.0 0.3 collective-permute-start
  11.2 35.9 %collective-permute-done = bf16[256,3072]{1,0:T(8,128)(2,1)S(1)} collective-permute-done((bf16[256,3072]{1,0:T(8,128)(2,1)S(1)}, bf16[256,3072]{1,0:T(8,128)(2,1)S(1)}, u32[]{:S(2)}, u32[]{:S(2)}) %collective-permute-start) | collective-permute-done | bytes 1572896 | tf_op jit(solution)/shard_map/ppermute | solution.py:24
  47.2 2.1 collective-permute-start.1
  49.2 33.4 %collective-permute-done.1 = bf16[256,3072]{1,0:T(8,128)(2,1)} collective-permute-done((bf16[256,3072]{1,0:T(8,128)(2,1)S(1)}, bf16[256,3072]{1,0:T(8,128)(2,1)}, u32[]{:S(2)}, u32[]{:S(2)}) %collective-permute-start.1) | collective-permute-done | bytes 1572896 | tf_op jit(solution)/shard_map/ppermute | solution.py:24
  82.6 3.8 %collective-permute-start.2 = (bf16[256,3072]{1,0:T(8,128)(2,1)}, bf16[256,3072]{1,0:T(8,128)(2,1)}, u32[]{:S(2)}, u32[]{:S(2)}) collective-permute-start(bf16[256,3072]{1,0:T(8,128)(2,1)} %collective-permute-done.1), channel_id=1, source_target_pairs={{0,1},{1,2},{2,3},{3,0},{4,5},{5,6},{6,7},{7,4},{8,9},{9,10},{10,1... | collective-permute-start | bytes 4718600 | tf_op jit(solution)/shard_map/ppermute | solution.py:24
  86.5 0.0 all-gather.5.cloned.1.call-update
  86.5 0.0 reduce-scatter.2.cloned.1.call-start
  86.6 32.2 %collective-permute-done.2 = bf16[256,3072]{1,0:T(8,128)(2,1)} collective-permute-done((bf16[256,3072]{1,0:T(8,128)(2,1)}, bf16[256,3072]{1,0:T(8,128)(2,1)}, u32[]{:S(2)}, u32[]{:S(2)}) %collective-permute-start.2) | collective-permute-done | bytes 1572896 | tf_op jit(solution)/shard_map/ppermute | solution.py:24
  118.8 2.7 constant_dynamic-update-slice_fusion.7
  121.5 2.7 constant_dynamic-update-slice_fusion.6
  124.1 1.3 constant_dynamic-update-slice_fusion.5
  125.4 1.9 constant_dynamic-update-slice_fusion.4
  127.3 2.7 constant_dynamic-update-slice_fusion.3
  130.0 2.7 constant_dynamic-update-slice_fusion.2
  132.7 1.3 constant_dynamic-update-slice_fusion.1
  134.0 2.0 constant_dynamic-update-slice_fusion
  136.0 19.6 %fusion.2 = f32[1024,2304]{0,1:T(8,128)S(1)} fusion(bf16[3072,2304]{1,0:T(8,128)(2,1)} %all-gather.3.cloned.1.call-done, bf16[2048,3072]{1,0:T(8,128)(2,1)} %constant_dynamic-update-slice_fusion, s32[]{:T(128)S(6)} %select_n.42), kind=kOutput, calls=%fused_computation.6 | convolution fusion | flops 14495514624 | bytes 29884420 | tf_op jit(solution)/shard_map/dot_general | solution.py:59
  155.6 3.5 %copy-done.3 = f32[1024,2304]{0,1:T(8,128)} copy-done((f32[1024,2304]{0,1:T(8,128)}, f32[1024,2304]{0,1:T(8,128)S(1)}, u32[]{:S(2)}) %copy-start.3) | copy-done | bytes 9437208
  159.2 2.1 slice.50
  161.3 3.5 %copy.21 = f32[1024,6,1,128]{3,0,1,2:T(8,128)} copy(f32[1024,6,1,128]{0,3,2,1:T(8,128)} %slice.50) | data formatting | bytes 6291456
  164.8 2.9 fusion.14
  167.8 2.3 multiply_reduce_fusion.1
  170.1 0.0 slice-start
  170.1 1.0 fusion.15
  171.1 0.0 slice-start.1
  171.1 0.0 slice-start.2
  171.1 8.2 %fusion = (f32[6,512]{1,0:T(8,128)S(1)}, f32[6,512,1024]{2,1,0:T(8,128)}) fusion(f32[1024,6,3,128]{0,3,2,1:T(8,128)} %bitcast.81, f32[1024,6]{0,1:T(8,128)S(1)} %add_rsqrt_fusion, bf16[1024,6,128]{2,0,1:T(8,128)(2,1)S(1)} %fusion.15), kind=kOutput, calls=%fused_computation.4 | convolution fusion | flops 813167616 | bytes 16560128 | tf_op jit(solution)/shard_map/qhe,khe->hqk/dot_general | solution.py:74
  179.3 2.7 fusion.1
  182.0 6.0 %fusion.21 = bf16[512,6,128]{0,2,1:T(8,128)(2,1)S(1)} fusion(f32[6,512,1024]{2,1,0:T(8,128)} %get-tuple-element.14, f32[6,512]{1,0:T(8,128)S(1)} %get-tuple-element.13, f32[1024,6,3,128]{0,3,2,1:T(8,128)S(1)} %bitcast.85), kind=kOutput, calls=%fused_computation.37 | convolution fusion | flops 815136768 | bytes 14958592 | tf_op jit(solution)/shard_map/hqk,khe->qhe/dot_general | solution.py:85
  188.0 2.9 fusion.22
  190.9 0.2 pad_maximum_fusion
  191.1 0.0 all-gather.5.cloned.1.call-done
  191.2 9.6 %convolution_convert_fusion = bf16[1024,3072]{1,0:T(8,128)(2,1)} fusion(bf16[1024,768]{0,1:T(8,128)(2,1)S(1)} %bitcast.87, bf16[768,3072]{1,0:T(8,128)(2,1)} %all-gather.5.cloned.1.call-done), kind=kOutput, calls=%fused_computation.10 | convolution fusion | flops 4834983936 | bytes 12582912 | tf_op jit(solution)/shard_map/dot_general | solution.py:91
  200.8 0.0 reduce-scatter.2.cloned.1.call-update
  201.6 111.6 %reduce-scatter.2.cloned.1.call-done = bf16[256,3072]{1,0:T(8,128)(2,1)} async-done(((bf16[1024,3072]{1,0:T(8,128)(2,1)}), bf16[256,3072]{1,0:T(8,128)(2,1)}) %reduce-scatter.2.cloned.1.call-update) | async-done | bytes 1572880 | tf_op jit(solution)/shard_map/reduce_scatter | solution.py:90
  313.2 0.0 copy-start.14
  313.2 2.1 fusion.16
  315.4 0.8 multiply_reduce_fusion
  316.2 1.1 bitcast_add_fusion
  317.3 1.9 collective-permute-start.3
  319.3 3.6 %collective-permute-start.5 = (bf16[256,128]{0,1:T(8,128)(2,1)S(1)}, bf16[256,128]{0,1:T(8,128)(2,1)S(1)}, u32[]{:S(2)}, u32[]{:S(2)}) collective-permute-start(bf16[256,128]{0,1:T(8,128)(2,1)S(1)} %fusion.29), channel_id=1, source_target_pairs={{4,0},{8,4},{12,8},{5,1},{9,5},{13,9},{6,2},{10,6},{14,10},{7,3},{... | collective-permute-start | bytes 196616 | tf_op jit(solution)/shard_map/ppermute | solution.py:34
  322.9 1.9 collective-permute-start.9
  324.8 2.4 collective-permute-start.7
  327.3 0.0 collective-permute-done.9
  327.3 1.3 collective-permute-start.10
  328.6 1.2 collective-permute-done.7
  329.7 4.3 %collective-permute-start.8 = (bf16[256]{0:T(256)(128)(2,1)S(1)}, bf16[256]{0:T(256)(128)(2,1)S(1)}, u32[]{:S(2)}, u32[]{:S(2)}) collective-permute-start(bf16[256]{0:T(256)(128)(2,1)S(1)} %collective-permute-done.7), channel_id=1, source_target_pairs={{2,0},{3,1},{6,4},{7,5},{10,8},{11,9},{14,12},{15,13},{18,16},{19,... | collective-permute-start | bytes 1544 | tf_op jit(solution)/shard_map/ppermute | solution.py:34
  334.0 0.0 collective-permute-done.3
  334.0 1.3 collective-permute-start.4
  335.3 0.0 collective-permute-done.5
  335.4 1.3 collective-permute-start.6
  336.7 0.0 collective-permute-done.8
  336.7 0.5 collective-permute-done.4
  337.2 5.2 %collective-permute-done.6 = bf16[256,128]{0,1:T(8,128)(2,1)S(1)} collective-permute-done((bf16[256,128]{0,1:T(8,128)(2,1)S(1)}, bf16[256,128]{0,1:T(8,128)(2,1)S(1)}, u32[]{:S(2)}, u32[]{:S(2)}) %collective-permute-start.6) | collective-permute-done | bytes 65568 | tf_op jit(solution)/shard_map/ppermute | solution.py:34
  342.5 0.7 slice_bitcast_fusion.1
  (43 shorter events, 0.2 us)
Async XLA Ops:
  7.2 309.0 %copy-start = (bf16[3072,64]{0,1:T(8,128)(2,1)S(1)}, bf16[3072,64]{0,1:T(8,128)(2,1)}, u32[]{:S(2)}) copy-start(bf16[3072,64]{0,1:T(8,128)(2,1)} %param.12) | copy-start | bytes 1179652
  7.2 1.5 copy-start.1
  7.2 2.3 copy-start.8
  7.2 128.8 %all-gather.3.cloned.1.call-start = ((), (), s32[]{:S(2)}) async-start(), calls=%async_computation.1 | async-start | bytes 17694720 | tf_op jit(solution)/shard_map/all_gather | solution.py:61
  7.9 183.2 %all-gather.5.cloned.1.call-start = ((), (), s32[]{:S(2)}) async-start(), calls=%async_computation.2 | async-start | bytes 5898240 | tf_op jit(solution)/shard_map/all_gather | solution.py:64
  9.5 0.7 copy-start.9
  10.2 72.5 %copy-start.5 = (f32[1,3072]{1,0:T(1,128)}, f32[1,3072]{1,0:T(1,128)S(1)}, u32[]{:S(2)}) copy-start(f32[1,3072]{1,0:T(1,128)S(1)} %get-tuple-element.8) | copy-start | bytes 36868
  11.0 36.2 %collective-permute-start = (bf16[256,3072]{1,0:T(8,128)(2,1)S(1)}, bf16[256,3072]{1,0:T(8,128)(2,1)S(1)}, u32[]{:S(2)}, u32[]{:S(2)}) collective-permute-start(bf16[256,3072]{1,0:T(8,128)(2,1)S(1)} %fusion.13), channel_id=1, source_target_pairs={{0,1},{1,2},{2,3},{3,0},{4,5},{5,6},{6,7},{7,4},{8,9},{9,10},{10,1... | collective-permute-start | bytes 4718600 | tf_op jit(solution)/shard_map/ppermute | solution.py:24
  47.2 35.5 %collective-permute-start.1 = (bf16[256,3072]{1,0:T(8,128)(2,1)S(1)}, bf16[256,3072]{1,0:T(8,128)(2,1)}, u32[]{:S(2)}, u32[]{:S(2)}) collective-permute-start(bf16[256,3072]{1,0:T(8,128)(2,1)S(1)} %collective-permute-done), channel_id=1, source_target_pairs={{0,1},{1,2},{2,3},{3,0},{4,5},{5,6},{6,7},{7,4},{8,9},{9,10},{10,1... | collective-permute-start | bytes 4718600 | tf_op jit(solution)/shard_map/ppermute | solution.py:24
  82.6 36.2 %collective-permute-start.2 = (bf16[256,3072]{1,0:T(8,128)(2,1)}, bf16[256,3072]{1,0:T(8,128)(2,1)}, u32[]{:S(2)}, u32[]{:S(2)}) collective-permute-start(bf16[256,3072]{1,0:T(8,128)(2,1)} %collective-permute-done.1), channel_id=1, source_target_pairs={{0,1},{1,2},{2,3},{3,0},{4,5},{5,6},{6,7},{7,4},{8,9},{9,10},{10,1... | collective-permute-start | bytes 4718600 | tf_op jit(solution)/shard_map/ppermute | solution.py:24
  86.5 226.7 %reduce-scatter.2.cloned.1.call-start = ((), (), s32[]{:S(2)}) async-start(), calls=%async_computation.3 | async-start | bytes 7864320 | tf_op jit(solution)/shard_map/reduce_scatter | solution.py:90
  121.5 3.9 %copy-start.6 = (f32[1,3072]{1,0:T(1,128)S(1)}, f32[1,3072]{1,0:T(1,128)}, u32[]{:S(2)}) copy-start(f32[1,3072]{1,0:T(1,128)} %copy-done.5) | copy-start | bytes 36868
  121.5 3.9 %copy-start.10 = (f32[256]{0:T(256)S(1)}, f32[256]{0:T(256)}, u32[]{:S(2)}) copy-start(f32[256]{0:T(256)} %copy-done.9) | copy-start | bytes 3076
  155.6 3.6 %copy-start.3 = (f32[1024,2304]{0,1:T(8,128)}, f32[1024,2304]{0,1:T(8,128)S(1)}, u32[]{:S(2)}) copy-start(f32[1024,2304]{0,1:T(8,128)S(1)} %fusion.2) | copy-start | bytes 28311556
  164.8 5.3 %copy-start.2 = (f32[1024,6,1,128]{3,0,1,2:T(8,128)S(1)}, f32[1024,6,1,128]{3,0,1,2:T(8,128)}, u32[]{:S(2)}) copy-start(f32[1024,6,1,128]{3,0,1,2:T(8,128)} %copy.21) | copy-start | bytes 9437188
  170.1 9.2 %slice-start = ((s8[9437184]{0:T(1024)(128)(4,1)}), s8[4194304]{0:T(1024)(128)(4,1)S(1)}, s32[]{:S(2)}) async-start(s8[9437184]{0:T(1024)(128)(4,1)} %bitcast.82), calls=%async_computation.4 | async-start | bytes 8388608
  171.1 8.2 %slice-start.1 = ((s8[9437184]{0:T(1024)(128)(4,1)}), s8[4194304]{0:T(1024)(128)(4,1)S(1)}, s32[]{:S(2)}) async-start(s8[9437184]{0:T(1024)(128)(4,1)} %bitcast.82), calls=%async_computation.5 | async-start | bytes 8388608
  171.1 8.2 %slice-start.2 = ((s8[9437184]{0:T(1024)(128)(4,1)}), s8[1048576]{0:T(1024)(128)(4,1)S(1)}, s32[]{:S(2)}) async-start(s8[9437184]{0:T(1024)(128)(4,1)} %bitcast.82), calls=%async_computation.6 | async-start | bytes 2097152
  200.8 0.7 copy-start.13
  200.8 112.4 %copy-start.7 = (f32[1,3072]{1,0:T(1,128)S(1)}, f32[1,3072]{1,0:T(1,128)}, u32[]{:S(2)}) copy-start(f32[1,3072]{1,0:T(1,128)} %get-tuple-element.6) | copy-start | bytes 36868
  313.2 2.2 copy-start.4
  313.2 3.0 copy-start.11
  313.2 3.0 copy-start.12
  313.2 3.0 copy-start.14
  317.3 16.7 %collective-permute-start.3 = (bf16[256,128]{0,1:T(8,128)(2,1)S(1)}, bf16[256,128]{0,1:T(8,128)(2,1)S(1)}, u32[]{:S(2)}, u32[]{:S(2)}) collective-permute-start(bf16[256,128]{0,1:T(8,128)(2,1)S(1)} %fusion.29), channel_id=1, source_target_pairs={{0,4},{4,8},{8,12},{1,5},{5,9},{9,13},{2,6},{6,10},{10,14},{3,7},{... | collective-permute-start | bytes 196616 | tf_op jit(solution)/shard_map/ppermute | solution.py:34
  319.3 16.1 %collective-permute-start.5 = (bf16[256,128]{0,1:T(8,128)(2,1)S(1)}, bf16[256,128]{0,1:T(8,128)(2,1)S(1)}, u32[]{:S(2)}, u32[]{:S(2)}) collective-permute-start(bf16[256,128]{0,1:T(8,128)(2,1)S(1)} %fusion.29), channel_id=1, source_target_pairs={{4,0},{8,4},{12,8},{5,1},{9,5},{13,9},{6,2},{10,6},{14,10},{7,3},{... | collective-permute-start | bytes 196616 | tf_op jit(solution)/shard_map/ppermute | solution.py:34
  322.9 4.3 %collective-permute-start.9 = (bf16[256]{0:T(256)(128)(2,1)S(1)}, bf16[256]{0:T(256)(128)(2,1)S(1)}, u32[]{:S(2)}, u32[]{:S(2)}) collective-permute-start(bf16[256]{0:T(256)(128)(2,1)S(1)} %convert_element_type.109), channel_id=1, source_target_pairs={{4,0},{8,4},{12,8},{5,1},{9,5},{13,9},{6,2},{10,6},{14,10},{7,3},{... | collective-permute-start | bytes 1544 | tf_op jit(solution)/shard_map/ppermute | solution.py:34
  324.8 4.9 %collective-permute-start.7 = (bf16[256]{0:T(256)(128)(2,1)S(1)}, bf16[256]{0:T(256)(128)(2,1)S(1)}, u32[]{:S(2)}, u32[]{:S(2)}) collective-permute-start(bf16[256]{0:T(256)(128)(2,1)S(1)} %convert_element_type.109), channel_id=1, source_target_pairs={{0,4},{4,8},{8,12},{1,5},{5,9},{9,13},{2,6},{6,10},{10,14},{3,7},{... | collective-permute-start | bytes 1544 | tf_op jit(solution)/shard_map/ppermute | solution.py:34
  327.3 9.4 %collective-permute-start.10 = (bf16[256]{0:T(256)(128)(2,1)S(1)}, bf16[256]{0:T(256)(128)(2,1)S(1)}, u32[]{:S(2)}, u32[]{:S(2)}) collective-permute-start(bf16[256]{0:T(256)(128)(2,1)S(1)} %collective-permute-done.9), channel_id=1, source_target_pairs={{0,2},{1,3},{4,6},{5,7},{8,10},{9,11},{12,14},{13,15},{16,18},{17,... | collective-permute-start | bytes 1544 | tf_op jit(solution)/shard_map/ppermute | solution.py:34
  329.7 6.9 %collective-permute-start.8 = (bf16[256]{0:T(256)(128)(2,1)S(1)}, bf16[256]{0:T(256)(128)(2,1)S(1)}, u32[]{:S(2)}, u32[]{:S(2)}) collective-permute-start(bf16[256]{0:T(256)(128)(2,1)S(1)} %collective-permute-done.7), channel_id=1, source_target_pairs={{2,0},{3,1},{6,4},{7,5},{10,8},{11,9},{14,12},{15,13},{18,16},{19,... | collective-permute-start | bytes 1544 | tf_op jit(solution)/shard_map/ppermute | solution.py:34
  334.0 3.2 collective-permute-start.4
  335.4 7.1 %collective-permute-start.6 = (bf16[256,128]{0,1:T(8,128)(2,1)S(1)}, bf16[256,128]{0,1:T(8,128)(2,1)S(1)}, u32[]{:S(2)}, u32[]{:S(2)}) collective-permute-start(bf16[256,128]{0,1:T(8,128)(2,1)S(1)} %collective-permute-done.5), channel_id=1, source_target_pairs={{0,2},{1,3},{4,6},{5,7},{8,10},{9,11},{12,14},{13,15},{16,18},{17,... | collective-permute-start | bytes 196616 | tf_op jit(solution)/shard_map/ppermute | solution.py:34
Sparse Core Ops, SparseCore 0:
  9.6 91.0 all-gather.2
  102.2 37.4 all-gather.4
  200.9 112.2 reduce-scatter.1
